TPU v7x, 128 devices: a whole 4x4x4 slice. The times are simulated.
128 devices in a mesh: outer: 4 (over z_lo, core), inner: 32 (over z_hi, y, x).
Axes of the slice: x: 4, y: 4, z: 4 (z_hi: 2, z_lo: 2; z = z_hi * 2 + z_lo), core: 2. Of those that a mesh axis runs over, the one named last changes fastest.
Arguments:
- inputs: bfloat16 [131072, 1024], P(('outer', 'inner')), may hold values from -24 to 24
- queries: bfloat16 [131072, 1024], P(('outer', 'inner')), may hold values from -6 to 6
- keys: bfloat16 [131072, 1024], P(('outer', 'inner')), may hold values from -6 to 6
- values: bfloat16 [131072, 1024], P(('outer', 'inner')), may hold values from -6 to 6
- out_grad: bfloat16 [131072, 1024], P(('outer', 'inner')), may hold values from -6 to 6
- master: float32 [1024, 1024], P('inner'), may hold values from -0.1875 to 0.1875
- moment1: float32 [1024, 1024], P('inner'), may hold values from -6 to 6
- moment2: float32 [1024, 1024], P('inner'), may hold values from 0.05 to 2
Outputs:
- query_grad: bfloat16 [131072, 1024], P(('outer', 'inner'))
- key_grad: bfloat16 [131072, 1024], P(('outer', 'inner'))
- new_master: float32 [1024, 1024], P('inner')
- new_moment1: float32 [1024, 1024], P('inner')
- new_moment2: float32 [1024, 1024], P('inner')
- weights: bfloat16 [1024, 1024], replicated
All inputs are finite; a program needn't handle non-finite values.
Results may differ from a plain program's by a relative error of at most 0.008.
Values may be sent and summed in bfloat16 or wider, within the bound.
A program may use at most 192 MiB of HBM per device.

v0:
```python
import math
import jax
import jax.numpy as jnp
from jax import lax
from jax.sharding import PartitionSpec as P

H = 8
HD = 128
BLK = 512


def entering(array, axis, combine, identity, reverse):
    count, place = (lax.axis_size(axis), lax.axis_index(axis))
    everything = lax.all_gather(array, axis)
    start = jnp.broadcast_to(jnp.asarray(identity, array.dtype), array.shape)

    def turn(k, before):
        at = count - 1 - k if reverse else k
        reached = at > place if reverse else at < place
        new = combine(before, everything[at])
        return jnp.where(reached, new, before)

    return lax.fori_loop(0, count, turn, start)


def add_states(earlier, later):
    return earlier + later


def split_state(state):
    upper = state.astype(jnp.bfloat16)
    lower = (state - upper.astype(jnp.float32)).astype(jnp.bfloat16)
    return (upper, lower)


def state_times_query(form, rows, state):
    upper, lower = split_state(state)
    first = jnp.einsum(form, rows, upper, preferred_element_type=jnp.float32)
    return first + jnp.einsum(form, rows, lower, preferred_element_type=jnp.float32)


def local(inputs, queries, keys, values, out_grad, master, moment1, moment2):
    rows_here = inputs.shape[0]
    width = inputs.shape[1]
    n_outer = lax.axis_size("outer")
    n_inner = lax.axis_size("inner")
    total_tokens = rows_here * n_outer * n_inner
    att_scale = 1.0 / math.sqrt(HD * total_tokens)
    grad_scale = 1.0 / math.sqrt(total_tokens)
    blocks = rows_here // BLK
    shape_four = (blocks, BLK, H, HD)
    query_blocks = queries.reshape(shape_four)
    key_blocks = keys.reshape(shape_four)
    value_blocks = values.reshape(shape_four)
    grad_blocks = out_grad.reshape(shape_four)
    kv_block = jnp.einsum(
        "nthk,nthv->nhkv", key_blocks, value_blocks, preferred_element_type=jnp.float32
    )
    qg_block = jnp.einsum(
        "nthv,nthk->nhvk", grad_blocks, query_blocks, preferred_element_type=jnp.float32
    )
    own_kv = jnp.sum(kv_block, 0)
    own_qg = jnp.sum(qg_block, 0)
    zero_state = jnp.zeros_like(own_kv)
    kv_earlier = entering(own_kv, ("outer", "inner"), add_states, zero_state, False)
    qg_later = entering(own_qg, ("outer", "inner"), add_states, zero_state, True)
    key_value_prior = kv_earlier[None] + jnp.concatenate(
        [zero_state[None], jnp.cumsum(kv_block, 0)[:-1]], 0
    )
    qg_reverse = jnp.cumsum(qg_block[::-1], 0)[::-1]
    qg_after = qg_later[None] + jnp.concatenate([qg_reverse[1:], zero_state[None]], 0)
    causal = jnp.arange(BLK)[:, None] >= jnp.arange(BLK)[None, :]
    query_parts = []
    key_parts = []
    for block_number in range(blocks):
        query_b = query_blocks[block_number]
        key_block_rows = key_blocks[block_number]
        value_block_rows = value_blocks[block_number]
        block_gradient = grad_blocks[block_number]
        scores = jnp.einsum(
            "thv,shv->hts", block_gradient, value_block_rows, preferred_element_type=jnp.float32
        )
        scores = jnp.where(causal[None], scores, 0.0).astype(jnp.bfloat16)
        query_gradient = jnp.einsum(
            "hts,shk->thk", scores, key_block_rows, preferred_element_type=jnp.float32
        )
        query_gradient = query_gradient + state_times_query(
            "rgn,gfn->rgf", block_gradient, key_value_prior[block_number]
        )
        dkey = jnp.einsum("hts,thk->shk", scores, query_b, preferred_element_type=jnp.float32)
        dkey = dkey + state_times_query("shv,hvk->shk", value_block_rows, qg_after[block_number])
        query_parts.append((query_gradient * att_scale).astype(jnp.bfloat16).reshape(BLK, width))
        key_parts.append((dkey * att_scale).astype(jnp.bfloat16).reshape(BLK, width))
    query_grad = jnp.concatenate(query_parts, 0)
    key_grad = jnp.concatenate(key_parts, 0)
    product = lax.dot_general(
        inputs, key_grad, (((0,), (0,)), ((), ())), preferred_element_type=jnp.float32
    )
    shares = lax.psum_scatter(product * grad_scale, "inner", scatter_dimension=0, tiled=True)
    grad = lax.psum(shares, "outer")
    new_moment1 = 0.9 * moment1 + 0.1 * grad
    new_moment2 = 0.95 * moment2 + 0.05 * grad * grad
    new_master = master - 0.01 * (new_moment1 / (jnp.sqrt(new_moment2) + 1e-08) + 0.1 * master)
    weights = lax.all_gather(new_master.astype(jnp.bfloat16), "inner", axis=0, tiled=True)
    return (query_grad, key_grad, new_master, new_moment1, new_moment2, weights)


def solution(mesh):
    in_specs = (
        P(("outer", "inner"), None),
        P(("outer", "inner"), None),
        P(("outer", "inner"), None),
        P(("outer", "inner"), None),
        P(("outer", "inner"), None),
        P("inner", None),
        P("inner", None),
        P("inner", None),
    )
    out_specs = (
        P(("outer", "inner"), None),
        P(("outer", "inner"), None),
        P("inner", None),
        P("inner", None),
        P("inner", None),
        P(),
    )
    return jax.shard_map(local, mesh=mesh, in_specs=in_specs, out_specs=out_specs, check_vma=False)
```

profile of v0, /device:TPU:1, one launch (start us, length us, event | category | flops | bytes accessed | tf_op | source)
XLA Modules:
  0.0 1391.0 jit_solution(7960946358874442010)
XLA Ops:
  7.2 2.4 copy.175
  10.2 2.9 fusion.43
  13.3 2.3 rev.4
  15.6 3.0 fusion.38
  18.6 2.3 copy.136
  20.9 2.3 copy.143
  23.2 3.0 fusion.40
  26.2 2.3 copy.170
  28.5 2.3 copy.172
  30.8 3.1 fusion.41
  33.8 2.3 copy.169
  36.1 2.3 copy.171
  38.5 5.1 select_convert_fusion
  43.6 3.4 select_convert_fusion.1
  47.0 353.1 %all-gather.10.cloned.1.call-done = f32[1024,128,128]{2,1,0:T(8,128)} async-done(((f32[8,128,128]{2,1,0:T(8,128)}), f32[1024,128,128]{2,1,0:T(8,128)}) %all-gather.10.cloned.1.call-update) | async-done | bytes 67108880 | tf_op jit(solution)/shard_map/all_gather | solution.py:14
  400.2 160.7 %while.31 = (s32[]{:T(128)}, f32[8,128,128]{2,1,0:T(8,128)S(1)}, s32[]{:T(128)}, f32[128,8,128,128]{3,2,1,0:T(8,128)}, s32[]{:T(128)}, /*index=5*/s32[]{:T(128)}, s32[]{:T(128)}, s32[]{:T(128)}) while((s32[]{:T(128)}, f32[8,128,128]{2,1,0:T(8,128)S(1)}, s32[]{:T(128)}, f32[128,8,128,128]{3,2,1,0:T(8,128)}, s32[]{:T(128)}, ...), condition=%wide.region_6.7_spmd.clone, body=%wide.region_5.6_spmd.clone.sunk | while | flops 393224 | bytes 1573027 | solution.py:23
  400.2 1.2 add_select_fusion.5
  560.9 1.5 fusion.14
  564.2 1.8 fusion.21
  566.0 1.8 fusion.28
  567.8 1.7 fusion.1
  569.5 2.4 copy.149
  571.9 5.2 fusion.3
  577.1 2.4 copy.148
  579.4 1.4 pad_maximum_fusion.1
  580.8 1.3 copy-done.19
  582.2 4.5 multiply_bitcast_fusion
  586.6 5.3 copy.167
  592.2 1.3 copy-done.12
  593.5 2.0 copy.174
  595.5 1.9 copy.173
  597.4 166.0 %reduce-scatter.4.cloned.1.call-done = f32[32,1024]{1,0:T(8,128)} async-done(((f32[1024,1024]{1,0:T(8,128)}), f32[32,1024]{1,0:T(8,128)}) %reduce-scatter.4.cloned.1.call-update) | async-done | bytes 131088 | tf_op jit(solution)/shard_map/reduce_scatter | solution.py:99
  763.5 3.5 fusion.42
  767.8 1.7 fusion.39
  769.5 1.3 copy.122
  771.4 48.4 %all-reduce.3.cloned.1.call-done = f32[32,1024]{1,0:T(8,128)} async-done(((f32[32,1024]{1,0:T(8,128)}), f32[32,1024]{1,0:T(8,128)}) %all-reduce.3.cloned.1.call-update) | async-done | bytes 131088 | tf_op jit(solution)/shard_map/psum | solution.py:100
  819.8 1.7 fusion.36
  821.5 384.5 %all-gather.8.cloned.1.call-done = f32[1024,128,128]{2,1,0:T(8,128)} async-done(((f32[8,128,128]{2,1,0:T(8,128)}), f32[1024,128,128]{2,1,0:T(8,128)}) %all-gather.8.cloned.1.call-update) | async-done | bytes 67108880 | tf_op jit(solution)/shard_map/all_gather | solution.py:14
  1206.0 160.2 %while.30 = (s32[]{:T(128)}, f32[8,128,128]{2,1,0:T(8,128)S(1)}, s32[]{:T(128)}, f32[128,8,128,128]{3,2,1,0:T(8,128)}, s32[]{:T(128)}, /*index=5*/s32[]{:T(128)}) while((s32[]{:T(128)}, f32[8,128,128]{2,1,0:T(8,128)S(1)}, s32[]{:T(128)}, f32[128,8,128,128]{3,2,1,0:T(8,128)}, s32[]{:T(128)}, /*index=5*/s32[]{:T(128)}) %tuple.83), condition=%wide.region_2.3_spmd.clone, body=%wide.region_1.0_spmd.clone.sunk | while | flops 393220 | bytes 1572965 | solution.py:23
  1259.8 1.2 add_select_fusion.4
  1273.6 1.2 add_select_fusion.4
  1368.2 1.3 copy-done.4
  1369.6 2.5 fusion.5
  1372.1 2.4 copy.135
  1375.3 1.3 copy-done.2
  1377.0 1.5 fusion.7
  1379.7 1.5 pad_maximum_fusion
  1381.2 3.2 copy.207
  (325 shorter events, 319.1 us)
Async XLA Ops:
  7.2 575.0 %copy-start = (bf16[1024,1024]{1,0:T(8,128)(2,1)S(1)}, bf16[1024,1024]{1,0:T(8,128)(2,1)}, u32[]{:S(2)}) copy-start(bf16[1024,1024]{1,0:T(8,128)(2,1)} %param.12) | copy-start | bytes 6291460
  7.2 393.0 %all-gather.10.cloned.1.call-start = ((), (), s32[]{:S(2)}) async-start(), calls=%async_computation.4 | async-start | bytes 67633152 | tf_op jit(solution)/shard_map/all_gather | solution.py:14
  7.2 2.4 copy-start.11
  13.2 750.2 %reduce-scatter.4.cloned.1.call-start = ((), (), s32[]{:S(2)}) async-start(), calls=%async_computation.5 | async-start | bytes 4325376 | tf_op jit(solution)/shard_map/reduce_scatter | solution.py:99
  38.5 5.1 copy-start.5
  38.5 5.1 copy-start.8
  400.2 160.7 %copy-start.24 = (pred[2]{0:T(512)(128)(4,1)S(1)}, pred[2]{0:T(512)(128)(4,1)}, u32[]{:S(2)}) copy-start(pred[2]{0:T(512)(128)(4,1)} %constant.95.clone.1) | copy-start | bytes 10
  560.9 1.5 copy-start.10
  562.9 1.2 copy-start.9
  564.2 3.6 copy-start.3
  566.0 1.8 copy-start.15
  569.5 2.4 copy-start.14
  577.1 2.4 copy-start.18
  580.8 1.3 copy-start.19
  591.9 1.6 copy-start.12
  592.0 227.8 %all-reduce.3.cloned.1.call-start = ((), (), s32[]{:S(2)}) async-start(), calls=%async_computation.1 | async-start | bytes 262144 | tf_op jit(solution)/shard_map/psum | solution.py:100
  593.5 2.0 copy-start.13
  595.5 168.0 %copy-start.20 = (bf16[128,8,8,128]{3,2,1,0:T(8,128)(2,1)S(1)}, bf16[128,8,8,128]{3,2,1,0:T(8,128)(2,1)}, u32[]{:S(2)}) copy-start(bf16[128,8,8,128]{3,2,1,0:T(8,128)(2,1)} %copy.174) | copy-start | bytes 6291460
  763.4 442.5 %all-gather.8.cloned.1.call-start = ((), (), s32[]{:S(2)}) async-start(), calls=%async_computation.3 | async-start | bytes 67633152 | tf_op jit(solution)/shard_map/all_gather | solution.py:14
  767.1 614.1 %all-gather.6.cloned.1.call-start = ((), (), s32[]{:S(2)}) async-start(), calls=%async_computation.2 | async-start | bytes 2162688 | tf_op jit(solution)/shard_map/all_gather | solution.py:104
  769.5 50.3 %copy-start.21 = (f32[32,1024]{1,0:T(8,128)S(1)}, f32[32,1024]{1,0:T(8,128)}, u32[]{:S(2)}) copy-start(f32[32,1024]{1,0:T(8,128)} %param.17) | copy-start | bytes 393220
  769.5 50.3 %copy-start.22 = (f32[32,1024]{1,0:T(8,128)S(1)}, f32[32,1024]{1,0:T(8,128)}, u32[]{:S(2)}) copy-start(f32[32,1024]{1,0:T(8,128)} %param.19) | copy-start | bytes 393220
  769.5 50.3 %copy-start.23 = (f32[32,1024]{1,0:T(8,128)S(1)}, f32[32,1024]{1,0:T(8,128)}, u32[]{:S(2)}) copy-start(f32[32,1024]{1,0:T(8,128)} %param.18) | copy-start | bytes 393220
  1366.2 1.2 copy-start.7
  1367.4 2.2 copy-start.4
  1372.1 2.4 copy-start.6
  1374.4 2.2 copy-start.2
  1374.8 2.2 copy-start.16
  1378.5 1.2 copy-start.17
  1381.2 3.2 copy-start.1
Sparse Core Ops, SparseCore 0:
  13.3 386.7 all-gather.9
  592.1 171.2 reduce-scatter.3
  765.9 53.8 all-reduce.2
  821.9 384.0 all-gather.7
  1208.9 70.3 all-gather.5
where the time goes:
time: 1400 us; the launch traced here: 1390 us
  waiting for transfers between devices  952 us (68%)
  other arithmetic  321 us (23%)
  local copies, waits for them, and re-layouts  60.2 us (4%)
  matrix products  36.5 us (3%)
  between operations  14.1 us (1%)
    all_gather x2, waiting for transfers between devices, entering(): everything = lax.all_gather(array, axis)  738 us
    select_n x256, other arithmetic, turn(): return jnp.where(reached, new, before)  314 us
    reduce_scatter x1, waiting for transfers between devices, local(): lax.psum_scatter(product * grad_scale, 'inner', scatter_dimension=0, tile...  166 us
    psum x1, waiting for transfers between devices, local(): grad = lax.psum(shares, 'outer')  48.4 us
    unnamed x60, local copies, waits for them, and re-layouts  33 us
  transfers between devices with their start and end apart: 5, of which 4 were waited for; matrix products, arithmetic and copies ran while one was open for 15% of the time, Pallas kernels for 0%

commit v1 on v0

--- a/solution.py
+++ b/solution.py
@@ -97,7 +97,8 @@
         inputs, key_grad, (((0,), (0,)), ((), ())), preferred_element_type=jnp.float32
     )
     shares = lax.psum_scatter(product * grad_scale, "inner", scatter_dimension=0, tiled=True)
-    grad = lax.psum(shares, "outer")
+    terms = lax.all_gather(shares, "outer")
+    grad = jnp.sum(terms, axis=0)
     new_moment1 = 0.9 * moment1 + 0.1 * grad
     new_moment2 = 0.95 * moment2 + 0.05 * grad * grad
     new_master = master - 0.01 * (new_moment1 / (jnp.sqrt(new_moment2) + 1e-08) + 0.1 * master)

time: 1400 us -> 1360 us (0.971)
  waiting for transfers between devices: 952 us -> 887 us
  blocking collectives: 0 us -> 30.1 us
    psum x1 -> x0, waiting for transfers between devices: 48.4 us -> none  [local(): grad = lax.psum(shares, 'outer')]
    all_gather x0 -> x1, blocking collectives: none -> 30.1 us  [local(): terms = lax.all_gather(shares, 'outer')]
    unnamed x60 -> x58, local copies, waits for them, and re-layouts: 33 us -> 31.4 us
  transfers between devices with their start and end apart: 5 -> 4, of which waited for: 4 -> 3; matrix products, arithmetic and copies ran while one was open for 15% -> 15% of each run, Pallas kernels for 0% -> 0%
where the time goes in v1:
time: 1360 us; the launch traced here: 1350 us
  waiting for transfers between devices  887 us (65%)
  other arithmetic  320 us (24%)
  local copies, waits for them, and re-layouts  58.6 us (4%)
  matrix products  34.9 us (3%)
  blocking collectives  30.1 us (2%)
  between operations  14.1 us (1%)
    all_gather x2, waiting for transfers between devices, entering(): everything = lax.all_gather(array, axis)  725 us
    select_n x256, other arithmetic, turn(): return jnp.where(reached, new, before)  314 us
    reduce_scatter x1, waiting for transfers between devices, local(): lax.psum_scatter(product * grad_scale, 'inner', scatter_dimension=0, tile...  161 us
    unnamed x58, local copies, waits for them, and re-layouts  31.4 us
    all_gather x1, blocking collectives, local(): terms = lax.all_gather(shares, 'outer')  30.1 us
  transfers between devices with their start and end apart: 4, of which 3 were waited for; matrix products, arithmetic and copies ran while one was open for 15% of the time, Pallas kernels for 0%

profile of v1, /device:TPU:1, one launch (start us, length us, event | category | flops | bytes accessed | tf_op | source)
XLA Modules:
  0.0 1351.9 jit_solution(8574302875787390313)
XLA Ops:
  7.2 2.4 copy.120
  10.2 2.9 fusion.43
  13.3 2.3 rev.4
  15.6 3.0 fusion.38
  18.7 2.3 copy.81
  20.9 2.3 copy.88
  23.2 3.0 fusion.40
  26.2 2.3 copy.115
  28.6 2.3 copy.117
  30.9 3.1 fusion.41
  33.9 2.3 copy.114
  36.3 2.3 copy.116
  38.7 5.1 select_convert_fusion
  43.7 3.4 select_convert_fusion.1
  47.1 353.0 %all-gather.11.cloned.1.call-done = f32[1024,128,128]{2,1,0:T(8,128)} async-done(((f32[8,128,128]{2,1,0:T(8,128)}), f32[1024,128,128]{2,1,0:T(8,128)}) %all-gather.11.cloned.1.call-update) | async-done | bytes 67108880 | tf_op jit(solution)/shard_map/all_gather | solution.py:14
  400.2 160.7 %while.31 = (s32[]{:T(128)}, f32[8,128,128]{2,1,0:T(8,128)S(1)}, s32[]{:T(128)}, f32[128,8,128,128]{3,2,1,0:T(8,128)}, s32[]{:T(128)}, /*index=5*/s32[]{:T(128)}, s32[]{:T(128)}, s32[]{:T(128)}) while((s32[]{:T(128)}, f32[8,128,128]{2,1,0:T(8,128)S(1)}, s32[]{:T(128)}, f32[128,8,128,128]{3,2,1,0:T(8,128)}, s32[]{:T(128)}, ...), condition=%wide.region_6.7_spmd.clone, body=%wide.region_5.6_spmd.clone.sunk | while | flops 393224 | bytes 1573027 | solution.py:23
  400.2 1.2 add_select_fusion.5
  560.9 1.5 fusion.14
  564.2 1.8 fusion.21
  566.0 1.8 fusion.28
  567.8 1.8 fusion.1
  569.6 2.4 copy.94
  571.9 5.2 fusion.3
  577.2 2.4 copy.93
  579.5 1.4 pad_maximum_fusion.1
  580.9 1.3 copy-done.19
  582.2 4.4 multiply_bitcast_fusion
  586.6 5.4 copy.112
  592.3 1.3 copy-done.12
  595.8 1.9 fusion.42
  598.4 1.7 fusion.39
  600.2 1.3 copy.67
  602.1 161.5 %reduce-scatter.4.cloned.1.call-done = f32[32,1024]{1,0:T(8,128)} async-done(((f32[1024,1024]{1,0:T(8,128)}), f32[32,1024]{1,0:T(8,128)}) %reduce-scatter.4.cloned.1.call-update) | async-done | bytes 131088 | tf_op jit(solution)/shard_map/reduce_scatter | solution.py:99
  763.5 30.1 %all-gather.2 = f32[128,1024]{1,0:T(8,128)S(1)} all-gather(f32[32,1024]{1,0:T(8,128)} %reduce-scatter.4.cloned.1.call-done), channel_id=4, replica_groups=mesh['outer'=4,'inner'=32] {'outer'}, dimensions={0}, use_global_device_ids=true | all-gather | bytes 655360 | tf_op jit(solution)/shard_map/all_gather | solution.py:100
  794.5 372.5 %all-gather.9.cloned.1.call-done = f32[1024,128,128]{2,1,0:T(8,128)} async-done(((f32[8,128,128]{2,1,0:T(8,128)}), f32[1024,128,128]{2,1,0:T(8,128)}) %all-gather.9.cloned.1.call-update) | async-done | bytes 67108880 | tf_op jit(solution)/shard_map/all_gather | solution.py:14
  1166.9 160.2 %while.30 = (s32[]{:T(128)}, f32[8,128,128]{2,1,0:T(8,128)S(1)}, s32[]{:T(128)}, f32[128,8,128,128]{3,2,1,0:T(8,128)}, s32[]{:T(128)}, /*index=5*/s32[]{:T(128)}) while((s32[]{:T(128)}, f32[8,128,128]{2,1,0:T(8,128)S(1)}, s32[]{:T(128)}, f32[128,8,128,128]{3,2,1,0:T(8,128)}, s32[]{:T(128)}, /*index=5*/s32[]{:T(128)}) %tuple.80), condition=%wide.region_2.3_spmd.clone, body=%wide.region_1.0_spmd.clone.sunk | while | flops 393220 | bytes 1572965 | solution.py:23
  1179.4 1.2 add_select_fusion.4
  1180.7 1.2 add_select_fusion.4
  1209.5 1.2 add_select_fusion.4
  1220.8 1.2 add_select_fusion.4
  1234.5 1.2 add_select_fusion.4
  1329.2 1.3 copy-done.4
  1330.5 2.5 fusion.5
  1333.0 2.4 copy.80
  1336.2 1.3 copy-done.2
  1338.0 1.5 fusion.7
  1340.7 1.5 pad_maximum_fusion
  1342.2 3.2 copy.151
  (322 shorter events, 318.3 us)
Async XLA Ops:
  7.2 575.1 %copy-start = (bf16[1024,1024]{1,0:T(8,128)(2,1)S(1)}, bf16[1024,1024]{1,0:T(8,128)(2,1)}, u32[]{:S(2)}) copy-start(bf16[1024,1024]{1,0:T(8,128)(2,1)} %param.12) | copy-start | bytes 6291460
  7.2 393.0 %all-gather.11.cloned.1.call-start = ((), (), s32[]{:S(2)}) async-start(), calls=%async_computation.3 | async-start | bytes 67633152 | tf_op jit(solution)/shard_map/all_gather | solution.py:14
  7.2 2.4 copy-start.11
  13.2 750.3 %reduce-scatter.4.cloned.1.call-start = ((), (), s32[]{:S(2)}) async-start(), calls=%async_computation.4 | async-start | bytes 4325376 | tf_op jit(solution)/shard_map/reduce_scatter | solution.py:99
  38.6 5.1 copy-start.5
  38.6 5.1 copy-start.8
  400.2 160.7 %copy-start.23 = (pred[2]{0:T(512)(128)(4,1)S(1)}, pred[2]{0:T(512)(128)(4,1)}, u32[]{:S(2)}) copy-start(pred[2]{0:T(512)(128)(4,1)} %constant.95.clone.1) | copy-start | bytes 10
  560.9 1.5 copy-start.10
  562.9 1.2 copy-start.9
  564.1 3.6 copy-start.3
  566.0 1.8 copy-start.15
  569.6 2.4 copy-start.14
  577.2 2.4 copy-start.18
  580.9 1.3 copy-start.19
  592.0 1.6 copy-start.12
  592.0 574.9 %all-gather.9.cloned.1.call-start = ((), (), s32[]{:S(2)}) async-start(), calls=%async_computation.2 | async-start | bytes 67633152 | tf_op jit(solution)/shard_map/all_gather | solution.py:14
  593.6 1.6 copy-start.13
  597.7 744.4 %all-gather.7.cloned.1.call-start = ((), (), s32[]{:S(2)}) async-start(), calls=%async_computation.1 | async-start | bytes 2162688 | tf_op jit(solution)/shard_map/all_gather | solution.py:105
  601.5 192.1 %copy-start.20 = (f32[32,1024]{1,0:T(8,128)S(1)}, f32[32,1024]{1,0:T(8,128)}, u32[]{:S(2)}) copy-start(f32[32,1024]{1,0:T(8,128)} %param.17) | copy-start | bytes 393220
  601.5 192.1 %copy-start.21 = (f32[32,1024]{1,0:T(8,128)S(1)}, f32[32,1024]{1,0:T(8,128)}, u32[]{:S(2)}) copy-start(f32[32,1024]{1,0:T(8,128)} %param.19) | copy-start | bytes 393220
  601.5 192.1 %copy-start.22 = (f32[32,1024]{1,0:T(8,128)S(1)}, f32[32,1024]{1,0:T(8,128)}, u32[]{:S(2)}) copy-start(f32[32,1024]{1,0:T(8,128)} %param.18) | copy-start | bytes 393220
  1327.1 1.2 copy-start.7
  1328.4 2.2 copy-start.4
  1333.0 2.4 copy-start.6
  1335.4 2.2 copy-start.2
  1335.8 2.2 copy-start.16
  1339.5 1.2 copy-start.17
  1342.2 3.2 copy-start.1
Sparse Core Ops, SparseCore 0:
  13.3 386.7 all-gather.10
  592.1 171.3 reduce-scatter.3
  765.8 401.1 all-gather.8
  1169.9 70.3 all-gather.6
